TPU v7x, 256 devices: a whole 4x4x8 slice. The times are simulated.
256 devices in a mesh: row: 64 (over y, x_hi, z), col: 4 (over x_lo, core).
Axes of the slice: x: 4 (x_hi: 2, x_lo: 2; x = x_hi * 2 + x_lo), y: 4, z: 8, core: 2. Of those that a mesh axis runs over, the one named last changes fastest.
Arguments:
- operator: bfloat16 [32768, 32768], P('row', 'col'), may hold values from -0.0068359375 to 0.0068359375
- rhs: float32 [32, 32768], P(None, 'row'), may hold values from -72 to 72
- bodies: int32 [32768], P('row'), may hold values from 0 to 63, as said below
- weights: float32 [32768], P('row'), may hold values from 0.5 to 1.5
Outputs:
- basis: float32 [128, 32768], P(None, ('row', 'col'))
- hess: float32 [128, 96], replicated
- start_factor: float32 [32, 32], replicated
Inputs may be any that keep to these rules, and one draw needn't show every extreme that they name: Every one of the 64 bodies has at least one node.
All inputs are finite; a program needn't handle non-finite values.
Results may differ from a plain program's by a relative error of at most 0.0025.
Values may be sent and summed in bfloat16 or wider, within the bound.
A program may use at most 64 MiB of HBM per device.

v0:
```python
import jax
import jax.numpy as jnp
from jax import lax
from jax.sharding import Mesh
from jax.sharding import PartitionSpec as P

N = 32768
S = 32
BODIES = 64
STEPS = 3
COL = ("col_0", "col_1")
ROW_COL = ("row_0", "row_1", "row_2", "col_0", "col_1")
ROW = ("row_0", "row_1", "row_2")


def one_axis_at_a_time(shard, axes):
    for axis in axes:
        shard = lax.psum(shard, axis)
    return shard


def joined_along(parts, dim):
    parts = jnp.moveaxis(parts, 0, dim)
    lengths = parts.shape
    return parts.reshape(*lengths[:dim], lengths[dim] * lengths[dim + 1], *lengths[dim + 2 :])


def all_blocks(shard, axes, sequence):
    parts = shard
    for k in sequence:
        parts = lax.all_gather(parts, axes[k])
    done = sequence[::-1]
    back = [done.index(k) for k in range(len(axes))]
    parts = parts.transpose(*back, *range(len(axes), parts.ndim))
    return parts.reshape(-1, *shard.shape)


def whole_of(shard, axes, sequence, dim):
    return joined_along(all_blocks(shard, axes, sequence), dim)


def sent_to_all(shard, axis):
    copies = jnp.broadcast_to(shard, (lax.axis_size(axis), *shard.shape))
    return lax.all_to_all(copies, axis, split_axis=0, concat_axis=0, tiled=True)


def over_copies(shard, axis):
    everything = sent_to_all(shard, axis)
    return jnp.sum(everything, axis=0)


def product_t(left, right):
    return lax.dot_general(
        left,
        right,
        (((1,), (1,)), ((), ())),
        precision=lax.Precision.HIGHEST,
        preferred_element_type=jnp.float32,
    )


def local(operator, rhs, bodies, weights):
    col_index = lax.axis_index(COL)
    col_count = lax.axis_size(COL)
    row_width = rhs.shape[1]
    quarter = row_width // col_count

    def portion(values):
        return lax.dynamic_slice_in_dim(values, col_index * quarter, quarter, 1)

    onehot = (bodies[:, None] == jnp.arange(BODIES, dtype=jnp.int32)[None, :]).astype(jnp.float32)
    onehot_part = jnp.transpose(portion(onehot.T))
    gram_start = one_axis_at_a_time(product_t(portion(rhs), portion(rhs)), ROW_COL) / N
    start_low = jnp.linalg.cholesky(gram_start)
    basis_list = [lax.linalg.triangular_solve(start_low, rhs, left_side=True, lower=True)]
    col_width = operator.shape[1]
    columns = []
    for step_index in range(STEPS):
        current = basis_list[-1]
        current_low = current.astype(jnp.bfloat16)
        gathered = whole_of(current_low, ROW, (1, 2, 0), 1)
        col_block = lax.dynamic_slice_in_dim(gathered, col_index * col_width, col_width, 1)
        partial_terms = lax.dot_general(
            col_block, operator, (((1,), (1,)), ((), ())), preferred_element_type=jnp.float32
        )
        coupled = over_copies(partial_terms, COL)
        scaled = current_low.astype(jnp.float32) * weights[None, :]
        body_partial = jnp.dot(portion(scaled), onehot_part, precision=lax.Precision.HIGHEST)
        body_means = one_axis_at_a_time(body_partial, ROW_COL) * (BODIES / N)
        completion = weights[None, :] * product_t(body_means, onehot)
        image_block = 0.5 * current + coupled + completion
        stacked = jnp.concatenate(basis_list, axis=0)
        stacked_part = portion(stacked)
        image_part = portion(image_block)
        coef_raw, gram_raw = (
            one_axis_at_a_time(product_t(stacked_part, image_part), ROW_COL),
            one_axis_at_a_time(product_t(image_part, image_part), ROW_COL),
        )
        first_coef = coef_raw / N
        residual_one = image_block - jnp.dot(first_coef.T, stacked, precision=lax.Precision.HIGHEST)
        gram_block = gram_raw / N - jnp.dot(
            first_coef.T, first_coef, precision=lax.Precision.HIGHEST
        )
        factor_low = jnp.linalg.cholesky(gram_block)
        basis_list.append(
            lax.linalg.triangular_solve(factor_low, residual_one, left_side=True, lower=True)
        )
        pieces = [first_coef, factor_low.T]
        below = (STEPS - 1 - step_index) * S
        if below > 0:
            pieces.append(jnp.zeros((below, S), jnp.float32))
        columns.append(jnp.concatenate(pieces, axis=0))
    basis = portion(jnp.concatenate(basis_list, axis=0))
    return (basis, jnp.concatenate(columns, axis=1), start_low)


def solution(mesh):
    split = Mesh(mesh.devices.reshape(4, 2, 8, 2, 2), ("row_0", "row_1", "row_2", "col_0", "col_1"))
    placed = (P(ROW, COL), P(None, ROW), P(ROW), P(ROW))
    return jax.shard_map(
        local, mesh=split, in_specs=placed, out_specs=(P(None, ROW_COL), P(), P()), check_vma=False
    )
```

profile of v0, /device:TPU:1, one launch (start us, length us, event | category | flops | bytes accessed | tf_op | source)
XLA Modules:
  0.0 710.6 jit_solution(9784179976770746269)
XLA Ops:
  8.2 14.2 %psum.350 = f32[32,32]{0,1:T(8,128)S(1)} all-reduce(f32[32,32]{0,1:T(8,128)S(1)} %fusion.50), channel_id=1, replica_groups=mesh['row_0'=4,'row_1'=2,'row_2'=8,'col_0'=2,'col_1'=2] {'row_0'}, use_global_device_ids=true, to_apply=%region_0.0 | all-reduce | flops 1024 | bytes 8192 | tf_op jit(solution)/shard_map/psum | solution.py:18
  22.4 9.1 %psum.351 = f32[32,32]{0,1:T(8,128)S(1)} all-reduce(f32[32,32]{0,1:T(8,128)S(1)} %psum.350), channel_id=1, replica_groups=mesh['row_0'=4,'row_1'=2,'row_2'=8,'col_0'=2,'col_1'=2] {'row_1'}, use_global_device_ids=true, to_apply=%region_1.0 | all-reduce | flops 1024 | bytes 8192 | tf_op jit(solution)/shard_map/psum | solution.py:18
  31.5 25.5 %psum.352 = f32[32,32]{0,1:T(8,128)S(1)} all-reduce(f32[32,32]{0,1:T(8,128)S(1)} %psum.351), channel_id=1, replica_groups=mesh['row_0'=4,'row_1'=2,'row_2'=8,'col_0'=2,'col_1'=2] {'row_2'}, use_global_device_ids=true, to_apply=%region_2.0 | all-reduce | flops 1024 | bytes 8192 | tf_op jit(solution)/shard_map/psum | solution.py:18
  57.0 5.2 psum.353
  62.2 18.9 %psum.354 = f32[32,32]{0,1:T(8,128)S(1)} all-reduce(f32[32,32]{0,1:T(8,128)S(1)} %psum.353), channel_id=1, replica_groups=mesh['row_0'=4,'row_1'=2,'row_2'=8,'col_0'=2,'col_1'=2] {'col_1'}, use_global_device_ids=true, to_apply=%region_4.0 | all-reduce | flops 1024 | bytes 8192 | tf_op jit(solution)/shard_map/psum | solution.py:18
  81.2 2.9 cholesky.74
  84.8 1.3 select_bitcast_fusion.3
  86.1 2.4 custom-call.8
  88.8 4.9 all-gather
  93.7 21.4 %all-gather.1 = bf16[16,32,512]{2,1,0:T(8,128)(2,1)} all-gather(bf16[2,32,512]{2,1,0:T(8,128)(2,1)S(1)} %bitcast.98), channel_id=3, replica_groups=mesh['row_0'=4,'row_1'=2,'row_2'=8,'col_0'=2,'col_1'=2] {'row_2'}, dimensions={0}, use_global_device_ids=true | all-gather | bytes 589824 | tf_op jit(solution)/shard_map/all_gather | solution.py:31
  115.9 0.8 iota_compare_fusion
  116.8 33.1 %all-gather.13.cloned.1.call-done = bf16[32,2,32,512]{3,2,1,0:T(8,128)(2,1)} async-done(((bf16[8,2,32,512]{3,2,1,0:T(8,128)(2,1)}), bf16[32,2,32,512]{3,2,1,0:T(8,128)(2,1)}) %all-gather.13.cloned.1.call-update) | async-done | bytes 2097168 | tf_op jit(solution)/shard_map/all_gather | solution.py:31
  149.9 2.0 copy.72
  152.0 1.9 copy-done.1
  153.9 2.6 fusion.7
  157.2 4.2 all-to-all-start
  161.6 11.2 %psum.355 = f32[32,64]{1,0:T(8,128)S(1)} all-reduce(f32[32,64]{1,0:T(8,128)S(1)} %fusion.24), channel_id=1, replica_groups=mesh['row_0'=4,'row_1'=2,'row_2'=8,'col_0'=2,'col_1'=2] {'row_0'}, use_global_device_ids=true, to_apply=%region_8.11 | all-reduce | flops 2048 | bytes 16384 | tf_op jit(solution)/shard_map/psum | solution.py:18
  172.8 9.1 %psum.356 = f32[32,64]{1,0:T(8,128)S(1)} all-reduce(f32[32,64]{1,0:T(8,128)S(1)} %psum.355), channel_id=1, replica_groups=mesh['row_0'=4,'row_1'=2,'row_2'=8,'col_0'=2,'col_1'=2] {'row_1'}, use_global_device_ids=true, to_apply=%region_9.12 | all-reduce | flops 2048 | bytes 16384 | tf_op jit(solution)/shard_map/psum | solution.py:18
  181.9 23.3 %psum.357 = f32[32,64]{1,0:T(8,128)S(1)} all-reduce(f32[32,64]{1,0:T(8,128)S(1)} %psum.356), channel_id=1, replica_groups=mesh['row_0'=4,'row_1'=2,'row_2'=8,'col_0'=2,'col_1'=2] {'row_2'}, use_global_device_ids=true, to_apply=%region_10.13 | all-reduce | flops 2048 | bytes 16384 | tf_op jit(solution)/shard_map/psum | solution.py:18
  205.2 5.9 psum.358
  211.0 18.1 %psum.359 = f32[32,64]{1,0:T(8,128)S(1)} all-reduce(f32[32,64]{1,0:T(8,128)S(1)} %psum.358), channel_id=1, replica_groups=mesh['row_0'=4,'row_1'=2,'row_2'=8,'col_0'=2,'col_1'=2] {'col_1'}, use_global_device_ids=true, to_apply=%region_12.15 | all-reduce | flops 2048 | bytes 16384 | tf_op jit(solution)/shard_map/psum | solution.py:18
  229.9 11.3 %all-reduce.5 = (f32[32,32]{0,1:T(8,128)S(1)}, f32[32,32]{0,1:T(8,128)S(1)}) all-reduce(f32[32,32]{0,1:T(8,128)S(1)} %fusion.45, f32[32,32]{0,1:T(8,128)S(1)} %fusion.59), channel_id=1, replica_groups=mesh['row_0'=4,'row_1'=2,'row_2'=8,'col_0'=2,'col_1'=2] {'row_0'}, use_global_device_ids=true, to_apply=%region_18.21 | all-reduce | flops 2048 | bytes 16384 | tf_op jit(solution)/shard_map/psum | solution.py:18
  241.2 8.1 %all-reduce.14 = (f32[32,32]{0,1:T(8,128)S(1)}, f32[32,32]{0,1:T(8,128)S(1)}) all-reduce(f32[32,32]{0,1:T(8,128)S(1)} %get-tuple-element.15, f32[32,32]{0,1:T(8,128)S(1)} %get-tuple-element.16), channel_id=1, replica_groups=mesh['row_0'=4,'row_1'=2,'row_2'=8,'col_0'=2,'col_1'=2] {'row_1'}, use_global_device_ids=true, to_apply=%region_19.22 | all-reduce | flops 2048 | bytes 16384 | tf_op jit(solution)/shard_map/psum | solution.py:18
  249.3 20.2 %all-reduce.2 = (f32[32,32]{0,1:T(8,128)S(1)}, f32[32,32]{0,1:T(8,128)S(1)}) all-reduce(f32[32,32]{0,1:T(8,128)S(1)} %get-tuple-element.33, f32[32,32]{0,1:T(8,128)S(1)} %get-tuple-element.34), channel_id=1, replica_groups=mesh['row_0'=4,'row_1'=2,'row_2'=8,'col_0'=2,'col_1'=2] {'row_2'}, use_global_device_ids=true, to_apply=%region_20.23 | all-reduce | flops 2048 | bytes 16384 | tf_op jit(solution)/shard_map/psum | solution.py:18
  269.4 5.5 all-reduce.11
  274.9 17.4 %all-reduce.8 = (f32[32,32]{0,1:T(8,128)S(1)}, f32[32,32]{0,1:T(8,128)S(1)}) all-reduce(f32[32,32]{0,1:T(8,128)S(1)} %get-tuple-element.27, f32[32,32]{0,1:T(8,128)S(1)} %get-tuple-element.28), channel_id=1, replica_groups=mesh['row_0'=4,'row_1'=2,'row_2'=8,'col_0'=2,'col_1'=2] {'col_1'}, use_global_device_ids=true, to_apply=%region_22.25 | all-reduce | flops 2048 | bytes 16384 | tf_op jit(solution)/shard_map/psum | solution.py:18
  292.8 2.9 cholesky.85
  297.0 2.4 custom-call.9
  299.8 4.9 all-gather.3
  304.7 21.7 %all-gather.4 = bf16[16,32,512]{2,1,0:T(8,128)(2,1)} all-gather(bf16[2,32,512]{2,1,0:T(8,128)(2,1)S(1)} %bitcast.99), channel_id=6, replica_groups=mesh['row_0'=4,'row_1'=2,'row_2'=8,'col_0'=2,'col_1'=2] {'row_2'}, dimensions={0}, use_global_device_ids=true | all-gather | bytes 589824 | tf_op jit(solution)/shard_map/all_gather | solution.py:31
  326.5 36.9 %all-gather.15.cloned.1.call-done = bf16[32,2,32,512]{3,2,1,0:T(8,128)(2,1)} async-done(((bf16[8,2,32,512]{3,2,1,0:T(8,128)(2,1)}), bf16[32,2,32,512]{3,2,1,0:T(8,128)(2,1)}) %all-gather.15.cloned.1.call-update) | async-done | bytes 2097168 | tf_op jit(solution)/shard_map/all_gather | solution.py:31
  363.4 1.8 copy.78
  365.4 6.0 fusion.5
  372.1 4.2 all-to-all-start.1
  376.4 11.2 %psum.370 = f32[32,64]{1,0:T(8,128)S(1)} all-reduce(f32[32,64]{1,0:T(8,128)S(1)} %fusion.22), channel_id=1, replica_groups=mesh['row_0'=4,'row_1'=2,'row_2'=8,'col_0'=2,'col_1'=2] {'row_0'}, use_global_device_ids=true, to_apply=%region_24.27 | all-reduce | flops 2048 | bytes 16384 | tf_op jit(solution)/shard_map/psum | solution.py:18
  387.7 9.1 %psum.371 = f32[32,64]{1,0:T(8,128)S(1)} all-reduce(f32[32,64]{1,0:T(8,128)S(1)} %psum.370), channel_id=1, replica_groups=mesh['row_0'=4,'row_1'=2,'row_2'=8,'col_0'=2,'col_1'=2] {'row_1'}, use_global_device_ids=true, to_apply=%region_25.28 | all-reduce | flops 2048 | bytes 16384 | tf_op jit(solution)/shard_map/psum | solution.py:18
  396.8 23.3 %psum.372 = f32[32,64]{1,0:T(8,128)S(1)} all-reduce(f32[32,64]{1,0:T(8,128)S(1)} %psum.371), channel_id=1, replica_groups=mesh['row_0'=4,'row_1'=2,'row_2'=8,'col_0'=2,'col_1'=2] {'row_2'}, use_global_device_ids=true, to_apply=%region_26.29 | all-reduce | flops 2048 | bytes 16384 | tf_op jit(solution)/shard_map/psum | solution.py:18
  420.0 5.9 psum.373
  425.9 18.1 %psum.374 = f32[32,64]{1,0:T(8,128)S(1)} all-reduce(f32[32,64]{1,0:T(8,128)S(1)} %psum.373), channel_id=1, replica_groups=mesh['row_0'=4,'row_1'=2,'row_2'=8,'col_0'=2,'col_1'=2] {'col_1'}, use_global_device_ids=true, to_apply=%region_28.31 | all-reduce | flops 2048 | bytes 16384 | tf_op jit(solution)/shard_map/psum | solution.py:18
  444.7 11.3 %all-reduce.4 = (f32[64,32]{0,1:T(8,128)S(1)}, f32[32,32]{0,1:T(8,128)S(1)}) all-reduce(f32[64,32]{0,1:T(8,128)S(1)} %fusion.18, f32[32,32]{0,1:T(8,128)S(1)} %fusion.56), channel_id=1, replica_groups=mesh['row_0'=4,'row_1'=2,'row_2'=8,'col_0'=2,'col_1'=2] {'row_0'}, use_global_device_ids=true, to_apply=%region_34.37 | all-reduce | flops 3072 | bytes 24576 | tf_op jit(solution)/shard_map/psum | solution.py:18
  456.1 8.1 %all-reduce.13 = (f32[64,32]{0,1:T(8,128)S(1)}, f32[32,32]{0,1:T(8,128)S(1)}) all-reduce(f32[64,32]{0,1:T(8,128)S(1)} %get-tuple-element.13, f32[32,32]{0,1:T(8,128)S(1)} %get-tuple-element.14), channel_id=1, replica_groups=mesh['row_0'=4,'row_1'=2,'row_2'=8,'col_0'=2,'col_1'=2] {'row_1'}, use_global_device_ids=true, to_apply=%region_35.38 | all-reduce | flops 3072 | bytes 24576 | tf_op jit(solution)/shard_map/psum | solution.py:18
  464.2 20.2 %all-reduce.1 = (f32[64,32]{0,1:T(8,128)S(1)}, f32[32,32]{0,1:T(8,128)S(1)}) all-reduce(f32[64,32]{0,1:T(8,128)S(1)} %get-tuple-element.31, f32[32,32]{0,1:T(8,128)S(1)} %get-tuple-element.32), channel_id=1, replica_groups=mesh['row_0'=4,'row_1'=2,'row_2'=8,'col_0'=2,'col_1'=2] {'row_2'}, use_global_device_ids=true, to_apply=%region_36.39 | all-reduce | flops 3072 | bytes 24576 | tf_op jit(solution)/shard_map/psum | solution.py:18
  484.3 5.5 all-reduce.10
  489.8 17.4 %all-reduce.7 = (f32[64,32]{0,1:T(8,128)S(1)}, f32[32,32]{0,1:T(8,128)S(1)}) all-reduce(f32[64,32]{0,1:T(8,128)S(1)} %get-tuple-element.25, f32[32,32]{0,1:T(8,128)S(1)} %get-tuple-element.26), channel_id=1, replica_groups=mesh['row_0'=4,'row_1'=2,'row_2'=8,'col_0'=2,'col_1'=2] {'col_1'}, use_global_device_ids=true, to_apply=%region_38.41 | all-reduce | flops 3072 | bytes 24576 | tf_op jit(solution)/shard_map/psum | solution.py:18
  507.6 2.9 cholesky.96
  511.9 2.4 custom-call.10
  514.6 4.9 all-gather.6
  519.6 21.7 %all-gather.7 = bf16[16,32,512]{2,1,0:T(8,128)(2,1)} all-gather(bf16[2,32,512]{2,1,0:T(8,128)(2,1)S(1)} %bitcast.100), channel_id=9, replica_groups=mesh['row_0'=4,'row_1'=2,'row_2'=8,'col_0'=2,'col_1'=2] {'row_2'}, dimensions={0}, use_global_device_ids=true | all-gather | bytes 589824 | tf_op jit(solution)/shard_map/all_gather | solution.py:31
  541.5 11.8 %psum.385 = f32[32,64]{1,0:T(8,128)S(1)} all-reduce(f32[32,64]{1,0:T(8,128)S(1)} %fusion.20), channel_id=1, replica_groups=mesh['row_0'=4,'row_1'=2,'row_2'=8,'col_0'=2,'col_1'=2] {'row_0'}, use_global_device_ids=true, to_apply=%region_40.43 | all-reduce | flops 2048 | bytes 16384 | tf_op jit(solution)/shard_map/psum | solution.py:18
  553.3 9.2 %psum.386 = f32[32,64]{1,0:T(8,128)S(1)} all-reduce(f32[32,64]{1,0:T(8,128)S(1)} %psum.385), channel_id=1, replica_groups=mesh['row_0'=4,'row_1'=2,'row_2'=8,'col_0'=2,'col_1'=2] {'row_1'}, use_global_device_ids=true, to_apply=%region_41.44 | all-reduce | flops 2048 | bytes 16384 | tf_op jit(solution)/shard_map/psum | solution.py:18
  562.5 22.1 %psum.387 = f32[32,64]{1,0:T(8,128)S(1)} all-reduce(f32[32,64]{1,0:T(8,128)S(1)} %psum.386), channel_id=1, replica_groups=mesh['row_0'=4,'row_1'=2,'row_2'=8,'col_0'=2,'col_1'=2] {'row_2'}, use_global_device_ids=true, to_apply=%region_42.45 | all-reduce | flops 2048 | bytes 16384 | tf_op jit(solution)/shard_map/psum | solution.py:18
  584.5 5.0 psum.388
  589.5 23.1 %psum.389 = f32[32,64]{1,0:T(8,128)S(1)} all-reduce(f32[32,64]{1,0:T(8,128)S(1)} %psum.388), channel_id=1, replica_groups=mesh['row_0'=4,'row_1'=2,'row_2'=8,'col_0'=2,'col_1'=2] {'col_1'}, use_global_device_ids=true, to_apply=%region_44.47 | all-reduce | flops 2048 | bytes 16384 | tf_op jit(solution)/shard_map/psum | solution.py:18
  612.7 1.8 copy.83
  614.7 6.0 fusion.3
  621.4 3.5 all-to-all-start.2
  625.0 5.2 all-to-all-done.2
  630.9 11.0 %all-reduce.3 = (f32[96,32]{0,1:T(8,128)S(1)}, f32[32,32]{0,1:T(8,128)S(1)}) all-reduce(f32[96,32]{0,1:T(8,128)S(1)} %fusion.15, f32[32,32]{0,1:T(8,128)S(1)} %fusion.53), channel_id=1, replica_groups=mesh['row_0'=4,'row_1'=2,'row_2'=8,'col_0'=2,'col_1'=2] {'row_0'}, use_global_device_ids=true, to_apply=%region_50.53 | all-reduce | flops 4096 | bytes 32768 | tf_op jit(solution)/shard_map/psum | solution.py:18
  641.9 9.1 %all-reduce.12 = (f32[96,32]{0,1:T(8,128)S(1)}, f32[32,32]{0,1:T(8,128)S(1)}) all-reduce(f32[96,32]{0,1:T(8,128)S(1)} %get-tuple-element.11, f32[32,32]{0,1:T(8,128)S(1)} %get-tuple-element.12), channel_id=1, replica_groups=mesh['row_0'=4,'row_1'=2,'row_2'=8,'col_0'=2,'col_1'=2] {'row_1'}, use_global_device_ids=true, to_apply=%region_51.54 | all-reduce | flops 4096 | bytes 32768 | tf_op jit(solution)/shard_map/psum | solution.py:18
  651.1 20.3 %all-reduce = (f32[96,32]{0,1:T(8,128)S(1)}, f32[32,32]{0,1:T(8,128)S(1)}) all-reduce(f32[96,32]{0,1:T(8,128)S(1)} %get-tuple-element.29, f32[32,32]{0,1:T(8,128)S(1)} %get-tuple-element.30), channel_id=1, replica_groups=mesh['row_0'=4,'row_1'=2,'row_2'=8,'col_0'=2,'col_1'=2] {'row_2'}, use_global_device_ids=true, to_apply=%region_52.55 | all-reduce | flops 4096 | bytes 32768 | tf_op jit(solution)/shard_map/psum | solution.py:18
  671.3 5.2 all-reduce.9
  676.5 18.7 %all-reduce.6 = (f32[96,32]{0,1:T(8,128)S(1)}, f32[32,32]{0,1:T(8,128)S(1)}) all-reduce(f32[96,32]{0,1:T(8,128)S(1)} %get-tuple-element.23, f32[32,32]{0,1:T(8,128)S(1)} %get-tuple-element.24), channel_id=1, replica_groups=mesh['row_0'=4,'row_1'=2,'row_2'=8,'col_0'=2,'col_1'=2] {'col_1'}, use_global_device_ids=true, to_apply=%region_54.57 | all-reduce | flops 4096 | bytes 32768 | tf_op jit(solution)/shard_map/psum | solution.py:18
  695.7 2.9 cholesky.107
  699.9 2.4 custom-call.11
  (77 shorter events, 15.5 us)
Async XLA Ops:
  7.2 0.8 copy-start
  7.2 142.7 %all-gather.13.cloned.1.call-start = ((), (), s32[]{:S(2)}) async-start(), calls=%async_computation.3 | async-start | bytes 2621440 | tf_op jit(solution)/shard_map/all_gather | solution.py:31
  149.9 4.0 copy-start.1
  153.9 75.3 %copy-start.2 = (s32[512]{0:T(512)S(1)}, s32[512]{0:T(512)}, u32[]{:S(2)}) copy-start(s32[512]{0:T(512)} %param.9) | copy-start | bytes 6148
  153.9 75.3 %copy-start.3 = (f32[512]{0:T(512)S(1)}, f32[512]{0:T(512)}, u32[]{:S(2)}) copy-start(f32[512]{0:T(512)} %param.10) | copy-start | bytes 6148
  157.2 71.9 %all-to-all-start = ((f32[4,32,512]{2,1,0:T(8,128)}), f32[4,32,512]{2,1,0:T(8,128)S(1)}, u32[]{:S(2)}, u32[]{:S(2)}) async-start(f32[4,32,512]{2,1,0:T(8,128)} %broadcast_in_dim.11), calls=%async_computation | async-start | bytes 524288 | tf_op jit(solution)/shard_map/all_to_all | solution.py:44
  161.4 201.9 %all-gather.15.cloned.1.call-start = ((), (), s32[]{:S(2)}) async-start(), calls=%async_computation.4 | async-start | bytes 2621440 | tf_op jit(solution)/shard_map/all_gather | solution.py:31
  372.1 71.9 %all-to-all-start.1 = ((f32[4,32,512]{2,1,0:T(8,128)}), f32[4,32,512]{2,1,0:T(8,128)S(1)}, u32[]{:S(2)}, u32[]{:S(2)}) async-start(f32[4,32,512]{2,1,0:T(8,128)} %broadcast_in_dim.12), calls=%async_computation.1 | async-start | bytes 524288 | tf_op jit(solution)/shard_map/all_to_all | solution.py:44
  376.3 236.4 %all-gather.17.cloned.1.call-start = ((), (), s32[]{:S(2)}) async-start(), calls=%async_computation.5 | async-start | bytes 2621440 | tf_op jit(solution)/shard_map/all_gather | solution.py:31
  621.4 8.8 %all-to-all-start.2 = ((f32[4,32,512]{2,1,0:T(8,128)}), f32[4,32,512]{2,1,0:T(8,128)S(1)}, u32[]{:S(2)}, u32[]{:S(2)}) async-start(f32[4,32,512]{2,1,0:T(8,128)} %broadcast_in_dim.13), calls=%async_computation.2 | async-start | bytes 524288 | tf_op jit(solution)/shard_map/all_to_all | solution.py:44
Sparse Core Ops, SparseCore 0:
  115.3 34.5 all-gather.12
  326.6 36.7 all-gather.14
  541.4 36.7 all-gather.16
where the time goes:
time: 712 us; the launch traced here: 711 us
  blocking collectives  548 us (77%)
  waiting for transfers between devices  75.4 us (11%)
  other arithmetic  29.6 us (4%)
  matrix products  19.3 us (3%)
  between operations  14.2 us (2%)
  local copies, waits for them, and re-layouts  12 us (2%)
  starting transfers between devices  12 us (2%)
    psum x35, blocking collectives, one_axis_at_a_time(): shard = lax.psum(shard, axis)  468 us
    all_gather x6, blocking collectives, all_blocks(): parts = lax.all_gather(parts, axes[k])  79.7 us
    all_gather x3, waiting for transfers between devices, all_blocks(): parts = lax.all_gather(parts, axes[k])  70.1 us
    dot_general x3, matrix products, local(): lax.dot_general(col_block, operator, (((1,), (1,)), ((), ())), preferred_...  14.6 us
  transfers between devices with their start and end apart: 6, of which 3 were waited for; matrix products, arithmetic and copies ran while one was open for 0% of the time, Pallas kernels for 0%

commit v1 on v0

--- a/solution.py
+++ b/solution.py
@@ -13,9 +13,15 @@
 ROW = ("row_0", "row_1", "row_2")
 
 
+def add_all(shard, name):
+    parts = lax.all_gather(shard, name, axis=0, tiled=False)
+    acc = parts.sum(axis=0)
+    return acc
+
+
 def one_axis_at_a_time(shard, axes):
     for axis in axes:
-        shard = lax.psum(shard, axis)
+        shard = add_all(shard, axis)
     return shard
 
 

time: 712 us -> 752 us (1.056)
  blocking collectives: 548 us -> 581 us
    all_gather x0 -> x50, blocking collectives: none -> 502 us  [add_all(): parts = lax.all_gather(shard, name, axis=0, tiled=False)]
    psum x35 -> x0, blocking collectives: 468 us -> none  [one_axis_at_a_time(): shard = lax.psum(shard, axis)]
where the time goes in v1:
time: 752 us; the launch traced here: 751 us
  blocking collectives  581 us (77%)
  waiting for transfers between devices  82.3 us (11%)
  other arithmetic  29.5 us (4%)
  matrix products  19.3 us (3%)
  between operations  14.3 us (2%)
  starting transfers between devices  12.2 us (2%)
  local copies, waits for them, and re-layouts  11.7 us (2%)
    all_gather x50, blocking collectives, add_all(): parts = lax.all_gather(shard, name, axis=0, tiled=False)  502 us
    all_gather x6, blocking collectives, all_blocks(): parts = lax.all_gather(parts, axes[k])  79.5 us
    all_gather x3, waiting for transfers between devices, all_blocks(): parts = lax.all_gather(parts, axes[k])  77.2 us
  transfers between devices with their start and end apart: 6, of which 3 were waited for; matrix products, arithmetic and copies ran while one was open for 0% of the time, Pallas kernels for 0%

profile of v1, /device:TPU:1, one launch (start us, length us, event | category | flops | bytes accessed | tf_op | source)
XLA Modules:
  0.0 750.6 jit_solution(16564965115281183012)
XLA Ops:
  8.2 10.4 %all-gather = f32[128,32]{1,0:T(8,128)S(1)} all-gather(f32[32,32]{1,0:T(8,128)S(1)} %fusion.48), channel_id=2, replica_groups=mesh['row_0'=4,'row_1'=2,'row_2'=8,'col_0'=2,'col_1'=2] {'row_0'}, dimensions={0}, use_global_device_ids=true | all-gather | bytes 20480 | tf_op jit(solution)/shard_map/all_gather | solution.py:17
  18.5 4.8 all-gather.1
  23.3 21.9 %all-gather.2 = f32[256,32]{1,0:T(8,128)S(1)} all-gather(f32[32,32]{1,0:T(8,128)S(1)} %reduce_sum.478), channel_id=4, replica_groups=mesh['row_0'=4,'row_1'=2,'row_2'=8,'col_0'=2,'col_1'=2] {'row_2'}, dimensions={0}, use_global_device_ids=true | all-gather | bytes 36864 | tf_op jit(solution)/shard_map/all_gather | solution.py:17
  45.2 3.5 all-gather.3
  48.8 13.3 %all-gather.4 = f32[64,32]{1,0:T(8,128)S(1)} all-gather(f32[32,32]{1,0:T(8,128)S(1)} %reduce_sum.480), channel_id=6, replica_groups=mesh['row_0'=4,'row_1'=2,'row_2'=8,'col_0'=2,'col_1'=2] {'col_1'}, dimensions={0}, use_global_device_ids=true | all-gather | bytes 12288 | tf_op jit(solution)/shard_map/all_gather | solution.py:17
  69.8 4.9 all-gather.5
  74.8 21.7 %all-gather.6 = bf16[16,32,512]{2,1,0:T(8,128)(2,1)} all-gather(bf16[2,32,512]{2,1,0:T(8,128)(2,1)S(1)} %bitcast.166), channel_id=8, replica_groups=mesh['row_0'=4,'row_1'=2,'row_2'=8,'col_0'=2,'col_1'=2] {'row_2'}, dimensions={0}, use_global_device_ids=true | all-gather | bytes 589824 | tf_op jit(solution)/shard_map/all_gather | solution.py:37
  96.8 38.4 %all-gather.73.cloned.1.call-done = bf16[32,2,32,512]{3,2,1,0:T(8,128)(2,1)} async-done(((bf16[8,2,32,512]{3,2,1,0:T(8,128)(2,1)}), bf16[32,2,32,512]{3,2,1,0:T(8,128)(2,1)}) %all-gather.73.cloned.1.call-update) | async-done | bytes 2097168 | tf_op jit(solution)/shard_map/all_gather | solution.py:37
  142.5 4.2 all-to-all-start
  146.8 9.0 %all-gather.8 = f32[128,64]{1,0:T(8,128)S(1)} all-gather(f32[32,64]{1,0:T(8,128)S(1)} %fusion.22), channel_id=10, replica_groups=mesh['row_0'=4,'row_1'=2,'row_2'=8,'col_0'=2,'col_1'=2] {'row_0'}, dimensions={0}, use_global_device_ids=true | all-gather | bytes 40960 | tf_op jit(solution)/shard_map/all_gather | solution.py:17
  155.9 4.8 all-gather.9
  160.6 20.0 %all-gather.10 = f32[256,64]{1,0:T(8,128)S(1)} all-gather(f32[32,64]{1,0:T(8,128)S(1)} %reduce_sum.484), channel_id=12, replica_groups=mesh['row_0'=4,'row_1'=2,'row_2'=8,'col_0'=2,'col_1'=2] {'row_2'}, dimensions={0}, use_global_device_ids=true | all-gather | bytes 73728 | tf_op jit(solution)/shard_map/all_gather | solution.py:17
  180.7 3.5 all-gather.11
  184.1 12.7 %all-gather.12 = f32[64,64]{1,0:T(8,128)S(1)} all-gather(f32[32,64]{1,0:T(8,128)S(1)} %reduce_sum.486), channel_id=14, replica_groups=mesh['row_0'=4,'row_1'=2,'row_2'=8,'col_0'=2,'col_1'=2] {'col_1'}, dimensions={0}, use_global_device_ids=true | all-gather | bytes 24576 | tf_op jit(solution)/shard_map/all_gather | solution.py:17
  197.5 9.0 %all-gather.18 = f32[128,32]{1,0:T(8,128)S(1)} all-gather(f32[32,32]{1,0:T(8,128)S(1)} %fusion.43), channel_id=20, replica_groups=mesh['row_0'=4,'row_1'=2,'row_2'=8,'col_0'=2,'col_1'=2] {'row_0'}, dimensions={0}, use_global_device_ids=true | all-gather | bytes 20480 | tf_op jit(solution)/shard_map/all_gather | solution.py:17
  206.5 4.8 all-gather.19
  211.2 18.5 %all-gather.20 = f32[256,32]{1,0:T(8,128)S(1)} all-gather(f32[32,32]{1,0:T(8,128)S(1)} %reduce_sum.494), channel_id=22, replica_groups=mesh['row_0'=4,'row_1'=2,'row_2'=8,'col_0'=2,'col_1'=2] {'row_2'}, dimensions={0}, use_global_device_ids=true | all-gather | bytes 36864 | tf_op jit(solution)/shard_map/all_gather | solution.py:17
  229.7 3.7 all-gather.21
  233.5 12.7 %all-gather.22 = f32[64,32]{1,0:T(8,128)S(1)} all-gather(f32[32,32]{1,0:T(8,128)S(1)} %reduce_sum.496), channel_id=24, replica_groups=mesh['row_0'=4,'row_1'=2,'row_2'=8,'col_0'=2,'col_1'=2] {'col_1'}, dimensions={0}, use_global_device_ids=true | all-gather | bytes 12288 | tf_op jit(solution)/shard_map/all_gather | solution.py:17
  246.4 9.0 %all-gather.13 = f32[128,32]{1,0:T(8,128)S(1)} all-gather(f32[32,32]{1,0:T(8,128)S(1)} %fusion.57), channel_id=15, replica_groups=mesh['row_0'=4,'row_1'=2,'row_2'=8,'col_0'=2,'col_1'=2] {'row_0'}, dimensions={0}, use_global_device_ids=true | all-gather | bytes 20480 | tf_op jit(solution)/shard_map/all_gather | solution.py:17
  255.4 4.8 all-gather.14
  260.2 18.5 %all-gather.15 = f32[256,32]{1,0:T(8,128)S(1)} all-gather(f32[32,32]{1,0:T(8,128)S(1)} %reduce_sum.489), channel_id=17, replica_groups=mesh['row_0'=4,'row_1'=2,'row_2'=8,'col_0'=2,'col_1'=2] {'row_2'}, dimensions={0}, use_global_device_ids=true | all-gather | bytes 36864 | tf_op jit(solution)/shard_map/all_gather | solution.py:17
  278.7 3.7 all-gather.16
  282.4 12.7 %all-gather.17 = f32[64,32]{1,0:T(8,128)S(1)} all-gather(f32[32,32]{1,0:T(8,128)S(1)} %reduce_sum.491), channel_id=19, replica_groups=mesh['row_0'=4,'row_1'=2,'row_2'=8,'col_0'=2,'col_1'=2] {'col_1'}, dimensions={0}, use_global_device_ids=true | all-gather | bytes 12288 | tf_op jit(solution)/shard_map/all_gather | solution.py:17
  302.4 4.9 all-gather.23
  307.3 21.5 %all-gather.24 = bf16[16,32,512]{2,1,0:T(8,128)(2,1)} all-gather(bf16[2,32,512]{2,1,0:T(8,128)(2,1)S(1)} %bitcast.167), channel_id=26, replica_groups=mesh['row_0'=4,'row_1'=2,'row_2'=8,'col_0'=2,'col_1'=2] {'row_2'}, dimensions={0}, use_global_device_ids=true | all-gather | bytes 589824 | tf_op jit(solution)/shard_map/all_gather | solution.py:37
  328.8 38.9 %all-gather.75.cloned.1.call-done = bf16[32,2,32,512]{3,2,1,0:T(8,128)(2,1)} async-done(((bf16[8,2,32,512]{3,2,1,0:T(8,128)(2,1)}), bf16[32,2,32,512]{3,2,1,0:T(8,128)(2,1)}) %all-gather.75.cloned.1.call-update) | async-done | bytes 2097168 | tf_op jit(solution)/shard_map/all_gather | solution.py:37
  369.7 6.0 fusion.5
  376.4 4.2 all-to-all-start.1
  380.8 9.0 %all-gather.26 = f32[128,64]{1,0:T(8,128)S(1)} all-gather(f32[32,64]{1,0:T(8,128)S(1)} %fusion.20), channel_id=28, replica_groups=mesh['row_0'=4,'row_1'=2,'row_2'=8,'col_0'=2,'col_1'=2] {'row_0'}, dimensions={0}, use_global_device_ids=true | all-gather | bytes 40960 | tf_op jit(solution)/shard_map/all_gather | solution.py:17
  389.8 4.8 all-gather.27
  394.6 20.0 %all-gather.28 = f32[256,64]{1,0:T(8,128)S(1)} all-gather(f32[32,64]{1,0:T(8,128)S(1)} %reduce_sum.500), channel_id=30, replica_groups=mesh['row_0'=4,'row_1'=2,'row_2'=8,'col_0'=2,'col_1'=2] {'row_2'}, dimensions={0}, use_global_device_ids=true | all-gather | bytes 73728 | tf_op jit(solution)/shard_map/all_gather | solution.py:17
  414.6 3.5 all-gather.29
  418.1 12.7 %all-gather.30 = f32[64,64]{1,0:T(8,128)S(1)} all-gather(f32[32,64]{1,0:T(8,128)S(1)} %reduce_sum.502), channel_id=32, replica_groups=mesh['row_0'=4,'row_1'=2,'row_2'=8,'col_0'=2,'col_1'=2] {'col_1'}, dimensions={0}, use_global_device_ids=true | all-gather | bytes 24576 | tf_op jit(solution)/shard_map/all_gather | solution.py:17
  431.4 9.0 %all-gather.59 = f32[4,64,32]{1,2,0:T(8,128)S(1)} all-gather(f32[1,64,32]{1,2,0:T(8,128)S(1)} %convolution_bitcast_fusion.1), channel_id=38, replica_groups=mesh['row_0'=4,'row_1'=2,'row_2'=8,'col_0'=2,'col_1'=2] {'row_0'}, dimensions={0}, use_global_device_ids=true | all-gather | bytes 40960 | tf_op jit(solution)/shard_map/all_gather | solution.py:17
  440.4 4.8 all-gather.60
  445.2 18.5 %all-gather.61 = f32[8,64,32]{1,2,0:T(8,128)S(1)} all-gather(f32[1,64,32]{1,2,0:T(8,128)S(1)} %bitcast.194), channel_id=40, replica_groups=mesh['row_0'=4,'row_1'=2,'row_2'=8,'col_0'=2,'col_1'=2] {'row_2'}, dimensions={0}, use_global_device_ids=true | all-gather | bytes 73728 | tf_op jit(solution)/shard_map/all_gather | solution.py:17
  463.7 3.7 all-gather.62
  467.4 12.7 %all-gather.63 = f32[2,64,32]{1,2,0:T(8,128)S(1)} all-gather(f32[1,64,32]{1,2,0:T(8,128)S(1)} %bitcast.196), channel_id=42, replica_groups=mesh['row_0'=4,'row_1'=2,'row_2'=8,'col_0'=2,'col_1'=2] {'col_1'}, dimensions={0}, use_global_device_ids=true | all-gather | bytes 24576 | tf_op jit(solution)/shard_map/all_gather | solution.py:17
  480.3 9.0 %all-gather.31 = f32[128,32]{1,0:T(8,128)S(1)} all-gather(f32[32,32]{1,0:T(8,128)S(1)} %fusion.54), channel_id=33, replica_groups=mesh['row_0'=4,'row_1'=2,'row_2'=8,'col_0'=2,'col_1'=2] {'row_0'}, dimensions={0}, use_global_device_ids=true | all-gather | bytes 20480 | tf_op jit(solution)/shard_map/all_gather | solution.py:17
  489.3 4.8 all-gather.32
  494.1 18.7 %all-gather.33 = f32[256,32]{1,0:T(8,128)S(1)} all-gather(f32[32,32]{1,0:T(8,128)S(1)} %reduce_sum.505), channel_id=35, replica_groups=mesh['row_0'=4,'row_1'=2,'row_2'=8,'col_0'=2,'col_1'=2] {'row_2'}, dimensions={0}, use_global_device_ids=true | all-gather | bytes 36864 | tf_op jit(solution)/shard_map/all_gather | solution.py:17
  512.7 3.7 all-gather.34
  516.5 12.7 %all-gather.35 = f32[64,32]{1,0:T(8,128)S(1)} all-gather(f32[32,32]{1,0:T(8,128)S(1)} %reduce_sum.507), channel_id=37, replica_groups=mesh['row_0'=4,'row_1'=2,'row_2'=8,'col_0'=2,'col_1'=2] {'col_1'}, dimensions={0}, use_global_device_ids=true | all-gather | bytes 12288 | tf_op jit(solution)/shard_map/all_gather | solution.py:17
  536.4 4.9 all-gather.41
  541.4 21.5 %all-gather.42 = bf16[16,32,512]{2,1,0:T(8,128)(2,1)} all-gather(bf16[2,32,512]{2,1,0:T(8,128)(2,1)S(1)} %bitcast.168), channel_id=44, replica_groups=mesh['row_0'=4,'row_1'=2,'row_2'=8,'col_0'=2,'col_1'=2] {'row_2'}, dimensions={0}, use_global_device_ids=true | all-gather | bytes 589824 | tf_op jit(solution)/shard_map/all_gather | solution.py:37
  563.0 9.0 %all-gather.44 = f32[128,64]{1,0:T(8,128)S(1)} all-gather(f32[32,64]{1,0:T(8,128)S(1)} %fusion.18), channel_id=46, replica_groups=mesh['row_0'=4,'row_1'=2,'row_2'=8,'col_0'=2,'col_1'=2] {'row_0'}, dimensions={0}, use_global_device_ids=true | all-gather | bytes 40960 | tf_op jit(solution)/shard_map/all_gather | solution.py:17
  572.1 4.8 all-gather.45
  576.8 20.2 %all-gather.46 = f32[256,64]{1,0:T(8,128)S(1)} all-gather(f32[32,64]{1,0:T(8,128)S(1)} %reduce_sum.516), channel_id=48, replica_groups=mesh['row_0'=4,'row_1'=2,'row_2'=8,'col_0'=2,'col_1'=2] {'row_2'}, dimensions={0}, use_global_device_ids=true | all-gather | bytes 73728 | tf_op jit(solution)/shard_map/all_gather | solution.py:17
  597.1 3.8 all-gather.47
  600.9 18.0 %all-gather.48 = f32[64,64]{1,0:T(8,128)S(1)} all-gather(f32[32,64]{1,0:T(8,128)S(1)} %reduce_sum.518), channel_id=50, replica_groups=mesh['row_0'=4,'row_1'=2,'row_2'=8,'col_0'=2,'col_1'=2] {'col_1'}, dimensions={0}, use_global_device_ids=true | all-gather | bytes 24576 | tf_op jit(solution)/shard_map/all_gather | solution.py:17
  620.9 6.0 fusion.3
  627.7 3.7 all-to-all-start.2
  631.4 5.0 all-to-all-done.2
  637.2 9.0 %all-gather.64 = f32[4,96,32]{1,2,0:T(8,128)S(1)} all-gather(f32[1,96,32]{1,2,0:T(8,128)S(1)} %convolution_bitcast_fusion), channel_id=56, replica_groups=mesh['row_0'=4,'row_1'=2,'row_2'=8,'col_0'=2,'col_1'=2] {'row_0'}, dimensions={0}, use_global_device_ids=true | all-gather | bytes 61440 | tf_op jit(solution)/shard_map/all_gather | solution.py:17
  646.2 4.8 all-gather.65
  650.9 18.8 %all-gather.66 = f32[8,96,32]{1,2,0:T(8,128)S(1)} all-gather(f32[1,96,32]{1,2,0:T(8,128)S(1)} %bitcast.198), channel_id=58, replica_groups=mesh['row_0'=4,'row_1'=2,'row_2'=8,'col_0'=2,'col_1'=2] {'row_2'}, dimensions={0}, use_global_device_ids=true | all-gather | bytes 110592 | tf_op jit(solution)/shard_map/all_gather | solution.py:17
  669.8 3.5 all-gather.67
  673.3 13.2 %all-gather.68 = f32[2,96,32]{1,2,0:T(8,128)S(1)} all-gather(f32[1,96,32]{1,2,0:T(8,128)S(1)} %bitcast.200), channel_id=60, replica_groups=mesh['row_0'=4,'row_1'=2,'row_2'=8,'col_0'=2,'col_1'=2] {'col_1'}, dimensions={0}, use_global_device_ids=true | all-gather | bytes 36864 | tf_op jit(solution)/shard_map/all_gather | solution.py:17
  686.8 9.0 %all-gather.49 = f32[128,32]{1,0:T(8,128)S(1)} all-gather(f32[32,32]{1,0:T(8,128)S(1)} %fusion.51), channel_id=51, replica_groups=mesh['row_0'=4,'row_1'=2,'row_2'=8,'col_0'=2,'col_1'=2] {'row_0'}, dimensions={0}, use_global_device_ids=true | all-gather | bytes 20480 | tf_op jit(solution)/shard_map/all_gather | solution.py:17
  695.8 4.8 all-gather.50
  700.5 18.3 %all-gather.51 = f32[256,32]{1,0:T(8,128)S(1)} all-gather(f32[32,32]{1,0:T(8,128)S(1)} %reduce_sum.521), channel_id=53, replica_groups=mesh['row_0'=4,'row_1'=2,'row_2'=8,'col_0'=2,'col_1'=2] {'row_2'}, dimensions={0}, use_global_device_ids=true | all-gather | bytes 36864 | tf_op jit(solution)/shard_map/all_gather | solution.py:17
  718.8 3.5 all-gather.52
  722.4 13.1 %all-gather.53 = f32[64,32]{1,0:T(8,128)S(1)} all-gather(f32[32,32]{1,0:T(8,128)S(1)} %reduce_sum.523), channel_id=55, replica_groups=mesh['row_0'=4,'row_1'=2,'row_2'=8,'col_0'=2,'col_1'=2] {'col_1'}, dimensions={0}, use_global_device_ids=true | all-gather | bytes 12288 | tf_op jit(solution)/shard_map/all_gather | solution.py:17
  (147 shorter events, 48.6 us)
Async XLA Ops:
  7.2 0.8 copy-start
  7.2 89.4 %copy-start.3 = (f32[512]{0:T(512)S(1)}, f32[512]{0:T(512)}, u32[]{:S(2)}) copy-start(f32[512]{0:T(512)} %param.10) | copy-start | bytes 6148
  7.2 89.5 %copy-start.2 = (s32[512]{0:T(512)S(1)}, s32[512]{0:T(512)}, u32[]{:S(2)}) copy-start(s32[512]{0:T(512)} %param.9) | copy-start | bytes 6148
  7.2 128.0 %all-gather.73.cloned.1.call-start = ((), (), s32[]{:S(2)}) async-start(), calls=%async_computation.3 | async-start | bytes 2621440 | tf_op jit(solution)/shard_map/all_gather | solution.py:37
  135.2 4.0 copy-start.1
  142.5 54.3 %all-to-all-start = ((f32[4,32,512]{2,1,0:T(8,128)}), f32[4,32,512]{2,1,0:T(8,128)S(1)}, u32[]{:S(2)}, u32[]{:S(2)}) async-start(f32[4,32,512]{2,1,0:T(8,128)} %broadcast_in_dim.11), calls=%async_computation | async-start | bytes 524288 | tf_op jit(solution)/shard_map/all_to_all | solution.py:50
  146.7 221.0 %all-gather.75.cloned.1.call-start = ((), (), s32[]{:S(2)}) async-start(), calls=%async_computation.4 | async-start | bytes 2621440 | tf_op jit(solution)/shard_map/all_gather | solution.py:37
  376.4 54.3 %all-to-all-start.1 = ((f32[4,32,512]{2,1,0:T(8,128)}), f32[4,32,512]{2,1,0:T(8,128)S(1)}, u32[]{:S(2)}, u32[]{:S(2)}) async-start(f32[4,32,512]{2,1,0:T(8,128)} %broadcast_in_dim.12), calls=%async_computation.1 | async-start | bytes 524288 | tf_op jit(solution)/shard_map/all_to_all | solution.py:50
  380.6 238.3 %all-gather.77.cloned.1.call-start = ((), (), s32[]{:S(2)}) async-start(), calls=%async_computation.5 | async-start | bytes 2621440 | tf_op jit(solution)/shard_map/all_gather | solution.py:37
  627.7 8.8 %all-to-all-start.2 = ((f32[4,32,512]{2,1,0:T(8,128)}), f32[4,32,512]{2,1,0:T(8,128)S(1)}, u32[]{:S(2)}, u32[]{:S(2)}) async-start(f32[4,32,512]{2,1,0:T(8,128)} %broadcast_in_dim.13), calls=%async_computation.2 | async-start | bytes 524288 | tf_op jit(solution)/shard_map/all_to_all | solution.py:50
Sparse Core Ops, SparseCore 0:
  96.7 38.4 all-gather.72
  329.0 38.6 all-gather.74
  563.0 38.6 all-gather.76
